TPU v7x, 32 devices: a whole 2x2x4 slice. The times are simulated.
32 devices in a mesh: groups: 2 (over y), seq: 4 (over z), heads: 2 (over x), sub: 2 (over core).
Axes of the slice: x: 2, y: 2, z: 4, core: 2. Of those that a mesh axis runs over, the one named last changes fastest.
Arguments:
- queries: bfloat16 [4096, 2048], P(('groups', 'seq', 'heads', 'sub')), parts along dimension 0, may hold values from -12.5 to 12.5
- new_keys: bfloat16 [4096, 2048], P(('groups', 'seq', 'heads', 'sub')), parts along dimension 0, may hold values from -5 to 5
- new_values: bfloat16 [4096, 2048], P(('groups', 'seq', 'heads', 'sub')), parts along dimension 0, may hold values from -5 to 5
- cache_keys: bfloat16 [8192, 2048], P(('groups', 'seq'), ('heads', 'sub')), parts along dimension 0, may hold values from -5 to 5
- cache_values: bfloat16 [8192, 2048], P(('groups', 'seq'), ('heads', 'sub')), parts along dimension 0, may hold values from -5 to 5
- selection: int32 [8, 16, 8], P(('groups', 'seq'), ('heads', 'sub')), parts along dimension 0, may hold values from 0 to 7, as said below
Outputs:
- attended: bfloat16 [4096, 2048], P(('groups', 'seq', 'heads', 'sub')), parts along dimension 0
There are 2 independent parts, one for each index of `groups`. A program takes and returns all parts, laid end to end along the dimension named above; each array names one. Nothing has to cross between parts.
Inputs may be any that keep to these rules, and one draw needn't show every extreme that they name: `selection`: every selected block precedes the span; the 8 blocks of one query block and head are different. For one index of seq and one index of heads+sub, of the 32 selections of that device's query blocks and heads (heads taken in order from index times 4), exactly 8 names a block held by each index of seq (blocks index * 2 to index * 2 + 1).
All inputs are finite; a program needn't handle non-finite values.
Results may differ from a plain program's by a relative error of at most 0.0023.
Values may be sent and summed in bfloat16 or wider, within the bound.
A program may use at most 128 MiB of HBM per device.

v0:
```python
import functools
import math

import jax
import jax.numpy as jnp
from jax import lax
from jax.experimental import pallas as pl
from jax.experimental.pallas import tpu as pltpu
from jax.sharding import PartitionSpec as P

HD = 128
BLOCK = 512


MESH = pl.DeviceIdType.MESH
AHEAD = 2
TILE = 256


def span_tile(rows, length):
    return min(length, max(rows, TILE))


def columns(head):
    return pl.ds(pl.multiple_of(head * HD, HD), HD)


def fused_kernel(
    seq_count, heads_size, sub_size, head_count,
    q_ref, k_ref, v_ref, ck_ref, cv_ref, out_ref,
    qall, kown, vown, kc, vc, vt, msg_in, st_in, msg_out, st_out, part, pst, fin,
    loc_sem, xq_send, xq_recv, xkv_send, xkv_recv, zq_send, zq_recv,
    m_send, m_recv, t_send, t_recv, o_send, o_recv, o_loc,
):
    peers = heads_size * sub_size
    rows, span_cols = q_ref.shape[0], head_count * HD
    length = rows * peers
    tile = span_tile(rows, length)
    halves, bands = length // tile, tile // rows
    chunks = head_count * halves
    cache_blocks = kc.shape[0] // BLOCK
    scaling = HD ** (-0.5) * math.log2(math.e)
    at_seq = lax.axis_index("seq")
    place = lax.axis_index("heads") * sub_size + lax.axis_index("sub")
    has_left, has_right = at_seq > 0, at_seq < seq_count - 1

    def peer_of(step):
        return lax.rem(place + step, peers)

    def peer_id(peer):
        return {"heads": peer // sub_size, "sub": lax.rem(peer, sub_size)}

    def band(index):
        return pl.ds(pl.multiple_of(index * rows, rows), rows)

    def slab(index):
        return pl.ds(pl.multiple_of(index * span_cols, span_cols), span_cols)

    def head_cols(peer, head):
        return pl.ds(pl.multiple_of(peer * span_cols + head * HD, HD), HD)

    barrier = pltpu.get_barrier_semaphore()
    for step in range(1, peers):
        pl.semaphore_signal(barrier, inc=1, device_id=peer_id(peer_of(step)), device_id_type=MESH)

    @pl.when(has_left)
    def _():
        pl.semaphore_signal(barrier, inc=1, device_id={"seq": at_seq - 1}, device_id_type=MESH)

    @pl.when(has_right)
    def _():
        pl.semaphore_signal(barrier, inc=1, device_id={"seq": at_seq + 1}, device_id_type=MESH)

    own = [
        pltpu.make_async_copy(
            q_ref.at[:, slab(place)], qall.at[at_seq, band(place), :], loc_sem.at[0]
        ),
        pltpu.make_async_copy(k_ref.at[:, slab(place)], kown.at[band(place), :], loc_sem.at[1]),
        pltpu.make_async_copy(v_ref.at[:, slab(place)], vown.at[band(place), :], loc_sem.at[2]),
        pltpu.make_async_copy(ck_ref, kc, loc_sem.at[3]),
        pltpu.make_async_copy(cv_ref, vc, loc_sem.at[4]),
    ]
    for copy in (own[0], own[4], own[3], own[1], own[2]):
        copy.start()
    sides = has_left.astype(jnp.int32) + has_right.astype(jnp.int32)
    pl.semaphore_wait(barrier, peers - 1 + sides)

    def spread_q(peer, head):
        return pltpu.make_async_remote_copy(
            src_ref=q_ref.at[:, head_cols(peer, head)],
            dst_ref=qall.at[at_seq, band(place), columns(head)],
            send_sem=xq_send.at[head, peer],
            recv_sem=xq_recv.at[head, place],
            device_id=peer_id(peer),
            device_id_type=MESH,
        )

    def landed_q(peer, head):
        return pltpu.make_async_remote_copy(
            src_ref=q_ref.at[:, head_cols(peer, head)],
            dst_ref=qall.at[at_seq, band(peer), columns(head)],
            send_sem=xq_send.at[head, peer],
            recv_sem=xq_recv.at[head, peer],
            device_id=peer_id(peer),
            device_id_type=MESH,
        )

    def spread_kv(which, peer, source):
        ref, buffer = ((k_ref, kown), (v_ref, vown))[which]
        return pltpu.make_async_remote_copy(
            src_ref=ref.at[:, slab(peer)],
            dst_ref=buffer.at[band(source), :],
            send_sem=xkv_send.at[which, peer],
            recv_sem=xkv_recv.at[which, source],
            device_id=peer_id(peer),
            device_id_type=MESH,
        )

    def span_of(chunk):
        return pl.ds(pl.multiple_of(lax.rem(chunk, halves) * tile, tile), tile)

    def pass_q(owner, chunk, direction):
        piece = qall.at[owner, span_of(chunk), columns(chunk // halves)]
        return pltpu.make_async_remote_copy(
            src_ref=piece,
            dst_ref=piece,
            send_sem=zq_send.at[direction, owner, chunk],
            recv_sem=zq_recv.at[owner, chunk],
            device_id={"seq": at_seq + 2 * direction - 1},
            device_id_type=MESH,
        )

    def pass_out(owner, head, direction):
        slot = owner + direction
        to = {"seq": at_seq + 2 * direction - 1}
        return (
            pltpu.make_async_remote_copy(
                src_ref=msg_out.at[owner, head], dst_ref=msg_in.at[slot, head],
                send_sem=m_send.at[owner, head], recv_sem=m_recv.at[slot, head],
                device_id=to, device_id_type=MESH,
            ),
            pltpu.make_async_remote_copy(
                src_ref=st_out.at[owner, head], dst_ref=st_in.at[slot, head],
                send_sem=t_send.at[owner, head], recv_sem=t_recv.at[slot, head],
                device_id=to, device_id_type=MESH,
            ),
        )

    def got_out(slot, head):
        to = {"seq": lax.rem(at_seq + 1, seq_count)}
        return (
            pltpu.make_async_remote_copy(
                src_ref=msg_out.at[0, head], dst_ref=msg_in.at[slot, head],
                send_sem=m_send.at[0, head], recv_sem=m_recv.at[slot, head],
                device_id=to, device_id_type=MESH,
            ),
            pltpu.make_async_remote_copy(
                src_ref=st_out.at[0, head], dst_ref=st_in.at[slot, head],
                send_sem=t_send.at[0, head], recv_sem=t_recv.at[slot, head],
                device_id=to, device_id_type=MESH,
            ),
        )

    def spread_out(peer, source, head):
        return pltpu.make_async_remote_copy(
            src_ref=fin.at[band(peer), columns(head)],
            dst_ref=out_ref.at[:, head_cols(source, head)],
            send_sem=o_send.at[head, peer],
            recv_sem=o_recv.at[head, source],
            device_id=peer_id(peer),
            device_id_type=MESH,
        )

    def keep_out(head):
        return pltpu.make_async_copy(
            fin.at[band(place), columns(head)],
            out_ref.at[:, head_cols(place, head)],
            o_loc.at[head],
        )

    def each_head(fn):
        pl.loop(0, head_count)(fn)

    @functools.partial(each_head)
    def _(head):
        for step in range(1, peers):
            spread_q(peer_of(step), head).start()

    for which in range(2):
        for step in range(1, peers):
            spread_kv(which, peer_of(step), place).start()

    def own_ready(chunk):
        for index in range(bands):
            peer = lax.rem(chunk, halves) * bands + index

            @pl.when(peer != place)
            def _(peer=peer):
                landed_q(peer, chunk // halves).wait_recv()

        for direction, there in ((0, has_left), (1, has_right)):
            @pl.when(there)
            def _(direction=direction):
                pass_q(at_seq, chunk, direction).start()

    own[0].wait()
    for chunk in range(min(AHEAD, chunks)):
        own_ready(chunk)
    own[4].wait()

    @functools.partial(each_head)
    def _(head):
        for block in range(cache_blocks):
            piece = vc[block * BLOCK:(block + 1) * BLOCK, columns(head)]
            vt[head, :, block * BLOCK:(block + 1) * BLOCK] = (
                piece.astype(jnp.float32).T.astype(jnp.bfloat16)
            )

    own[3].wait()

    def attend(keys, values_t, queries, causal):
        scores = lax.dot_general(
            keys, queries, (((1,), (1,)), ((), ())), preferred_element_type=jnp.float32
        )
        if causal is not None:
            scores = jnp.where(causal, scores, -jnp.inf)
        top = jnp.max(scores, axis=0, keepdims=True)
        weights = jnp.exp2((scores - top) * scaling)
        total = jnp.sum(weights, axis=0, keepdims=True)
        mixed = jnp.dot(
            values_t, weights.astype(jnp.bfloat16), preferred_element_type=jnp.float32
        )
        return mixed, top * scaling, total

    def join(a, b):
        top = jnp.maximum(a[1], b[1])
        fa, fb = jnp.exp2(a[1] - top), jnp.exp2(b[1] - top)
        return a[0] * fa + b[0] * fb, top, a[2] * fa + b[2] * fb

    def put_part(owner, chunk, result):
        part[owner, chunk] = result[0]
        pst[owner, chunk, 0:1] = result[1]
        pst[owner, chunk, 1:2] = result[2]

    def get_part(owner, chunk):
        return part[owner, chunk], pst[owner, chunk, 0:1], pst[owner, chunk, 1:2]

    def cached_part(owner, chunk):
        head = chunk // halves
        queries = qall[owner, span_of(chunk), columns(head)]
        result = None
        for block in range(cache_blocks):
            piece = attend(
                kc[block * BLOCK:(block + 1) * BLOCK, columns(head)],
                vt[head, :, block * BLOCK:(block + 1) * BLOCK],
                queries,
                None,
            )
            result = piece if result is None else join(result, piece)
        put_part(owner, chunk, result)

    def own_part(chunk):
        head = chunk // halves
        queries = qall[at_seq, span_of(chunk), columns(head)]
        for at in range(halves):
            @pl.when(lax.rem(chunk, halves) == at)
            def _(at=at):
                depth = (at + 1) * tile
                key_at = lax.broadcasted_iota(jnp.int32, (depth, tile), 0)
                query_at = lax.broadcasted_iota(jnp.int32, (depth, tile), 1) + at * tile
                values_t = vown[0:depth, columns(head)].astype(jnp.float32).T
                piece = attend(
                    kown[0:depth, columns(head)],
                    values_t.astype(jnp.bfloat16),
                    queries,
                    key_at <= query_at,
                )
                put_part(at_seq, chunk, join(piece, get_part(at_seq, chunk)))

    lanes = min(tile, 128)
    folds = tile // lanes

    def fold_stats(owner, chunk, which, row):
        for index in range(folds):
            st_out[owner, chunk, which * folds + index:which * folds + index + 1] = row[
                :, index * lanes:(index + 1) * lanes
            ]

    def unfold_stats(slot, chunk, which):
        rows_of = [
            st_in[slot, chunk, which * folds + index:which * folds + index + 1]
            for index in range(folds)
        ]
        return jnp.concatenate(rows_of, axis=1)

    def take_in(slot, owner, chunk):
        for copy in got_out(slot, chunk):
            copy.wait_recv()
        mixed = msg_in[slot, chunk].astype(jnp.float32) * unfold_stats(slot, chunk, 2)
        other = (mixed, unfold_stats(slot, chunk, 0), unfold_stats(slot, chunk, 1))
        put_part(owner, chunk, join(get_part(owner, chunk), other))

    def inside(index, limit):
        return jnp.logical_and(index >= 0, index < limit)

    def foreign(index):
        distance = index // 2 + 1
        direction = lax.rem(index, 2)
        return at_seq + (2 * direction - 1) * distance, direction, distance

    last = 2 * seq_count - 3

    @pl.loop(0, chunks + last)
    def _(turn):
        @pl.loop(0, 2 * (seq_count - 1))
        def _(index):
            owner, direction, distance = foreign(index)
            chunk = turn + 1 - distance

            @pl.when(jnp.logical_and(inside(owner, seq_count), inside(chunk, chunks)))
            def _():
                pass_q(owner, chunk, 0).wait_recv()
                onward = 1 - direction

                @pl.when(inside(at_seq + 2 * onward - 1, seq_count))
                def _():
                    pass_q(owner, chunk, onward).start()

        @pl.when(turn + AHEAD < chunks)
        def _():
            own_ready(turn + AHEAD)

        @pl.loop(0, 2 * (seq_count - 1))
        def _(back):
            owner, direction, distance = foreign(2 * (seq_count - 1) - 1 - back)
            chunk = turn + 1 - distance

            @pl.when(jnp.logical_and(inside(owner, seq_count), inside(chunk, chunks)))
            def _():
                cached_part(owner, chunk)

            chunk = turn - (last - distance)

            @pl.when(jnp.logical_and(inside(owner, seq_count), inside(chunk, chunks)))
            def _():
                @pl.when(inside(at_seq - 2 * direction + 1, seq_count))
                def _():
                    take_in(owner + direction, owner, chunk)

                mixed = part[owner, chunk]
                most = jnp.maximum(jnp.max(jnp.abs(mixed), axis=0, keepdims=True), 1e-30)
                msg_out[owner, chunk] = (
                    jnp.round(mixed * (32767.0 / most)).astype(jnp.int32).astype(jnp.int16)
                )
                fold_stats(owner, chunk, 0, pst[owner, chunk, 0:1])
                fold_stats(owner, chunk, 1, pst[owner, chunk, 1:2])
                fold_stats(owner, chunk, 2, most * (1.0 / 32767.0))
                for copy in pass_out(owner, chunk, direction):
                    copy.start()

        @pl.when(turn < chunks)
        def _():
            cached_part(at_seq, turn)

        @pl.when(turn == last - 1)
        def _():
            own[1].wait()
            own[2].wait()
            for which in range(2):
                for step in range(1, peers):
                    peer = peer_of(step)
                    spread_kv(which, peer, peer).wait_recv()

        @pl.when(inside(turn - (last - 1), chunks))
        def _():
            own_part(turn - (last - 1))

        @pl.when(turn >= last)
        def _():
            chunk = turn - last
            head = chunk // halves
            for side, there in ((1, has_left), (0, has_right)):
                @pl.when(there)
                def _(side=side):
                    take_in(at_seq + side, at_seq, chunk)

            done = part[at_seq, chunk] / pst[at_seq, chunk, 1:2]
            fin[span_of(chunk), columns(head)] = done.T.astype(jnp.bfloat16)
            for index in range(bands):
                peer = lax.rem(chunk, halves) * bands + index

                @pl.when(peer != place)
                def _(peer=peer):
                    spread_out(peer, place, head).start()

                @pl.when(peer == place)
                def _():
                    keep_out(head).start()

    @functools.partial(each_head)
    def _(head):
        for step in range(1, peers):
            peer = peer_of(step)
            spread_out(peer, peer, head).wait_recv()
            spread_out(peer, place, head).wait_send()
            spread_q(peer, head).wait_send()
        keep_out(head).wait()

    @pl.loop(0, chunks)
    def _(chunk):
        for direction, there in ((0, has_left), (1, has_right)):
            @pl.when(there)
            def _(direction=direction):
                pass_q(at_seq, chunk, direction).wait_send()

        @pl.loop(0, 2 * (seq_count - 1))
        def _(index):
            owner, direction, distance = foreign(index)

            @pl.when(inside(owner, seq_count))
            def _():
                for copy in pass_out(owner, chunk, direction):
                    copy.wait_send()
                onward = 1 - direction

                @pl.when(inside(at_seq + 2 * onward - 1, seq_count))
                def _():
                    pass_q(owner, chunk, onward).wait_send()

    for which in range(2):
        for step in range(1, peers):
            spread_kv(which, peer_of(step), place).wait_send()


def dense_body(queries, new_keys, new_values, cache_keys, cache_values):
    seq_count = lax.axis_size("seq")
    heads_size, sub_size = lax.axis_size("heads"), lax.axis_size("sub")
    peers = heads_size * sub_size
    rows, width = queries.shape
    cached, span_cols = cache_keys.shape
    head_count, length = span_cols // HD, rows * peers
    tile = span_tile(rows, length)
    chunks = head_count * (length // tile)
    lanes = min(tile, 128)
    stat_rows = -(-3 * (tile // lanes) // 8) * 8
    dma = pltpu.SemaphoreType.DMA
    anywhere = pl.BlockSpec(memory_space=pltpu.HBM)
    return pl.pallas_call(
        functools.partial(fused_kernel, seq_count, heads_size, sub_size, head_count),
        out_shape=jax.ShapeDtypeStruct((rows, width), jnp.bfloat16),
        in_specs=[anywhere] * 5,
        out_specs=pl.BlockSpec(memory_space=pltpu.VMEM),
        scratch_shapes=[
            pltpu.VMEM((seq_count, length, span_cols), jnp.bfloat16),
            pltpu.VMEM((length, span_cols), jnp.bfloat16),
            pltpu.VMEM((length, span_cols), jnp.bfloat16),
            pltpu.VMEM((cached, span_cols), jnp.bfloat16),
            pltpu.VMEM((cached, span_cols), jnp.bfloat16),
            pltpu.VMEM((head_count, HD, cached), jnp.bfloat16),
            pltpu.VMEM((seq_count + 1, chunks, HD, tile), jnp.int16),
            pltpu.VMEM((seq_count + 1, chunks, stat_rows, lanes), jnp.float32),
            pltpu.VMEM((seq_count, chunks, HD, tile), jnp.int16),
            pltpu.VMEM((seq_count, chunks, stat_rows, lanes), jnp.float32),
            pltpu.VMEM((seq_count, chunks, HD, tile), jnp.float32),
            pltpu.VMEM((seq_count, chunks, 8, tile), jnp.float32),
            pltpu.VMEM((length, span_cols), jnp.bfloat16),
            dma((5,)),
            dma((head_count, peers)),
            dma((head_count, peers)),
            dma((2, peers)),
            dma((2, peers)),
            dma((2, seq_count, chunks)),
            dma((seq_count, chunks)),
            dma((seq_count, chunks)),
            dma((seq_count + 1, chunks)),
            dma((seq_count, chunks)),
            dma((seq_count + 1, chunks)),
            dma((head_count, peers)),
            dma((head_count, peers)),
            dma((head_count,)),
        ],
        compiler_params=pltpu.CompilerParams(
            collective_id=0, has_side_effects=True, vmem_limit_bytes=60 * 1024 * 1024
        ),
    )(queries, new_keys, new_values, cache_keys, cache_values)


def order_ranks(owners):
    length = owners.shape[-1]
    counter = jnp.arange(length)
    earlier = counter[None, :] < counter[:, None]
    same_owner = owners[..., :, None] == owners[..., None, :]
    return jnp.sum(jnp.logical_and(same_owner, earlier), axis=-1)


def one_hot(values, length):
    return (values[..., None] == jnp.arange(length)).astype(jnp.float32)


def own_partial(query_blocks, key_blocks, value_blocks, scaling):
    scores = (
        jnp.einsum("bqhd,bkhd->bhqk", query_blocks, key_blocks, preferred_element_type=jnp.float32)
        * scaling
    )
    length = query_blocks.shape[1]
    causal = jnp.arange(length)[:, None] >= jnp.arange(length)[None, :]
    scores = jnp.where(causal, scores, -jnp.inf)
    highest = jnp.max(scores, axis=-1)
    weights = jnp.exp(scores - highest[..., None])
    totals = jnp.sum(weights, axis=-1)
    mixed = jnp.einsum(
        "bhqk,bkhd->bhqd",
        weights.astype(jnp.bfloat16),
        value_blocks,
        preferred_element_type=jnp.float32,
    )
    return (mixed, highest, totals)


def tile_partial(query_blocks, tile_pair, scaling):
    head_size = query_blocks.shape[-1]
    scores = (
        jnp.einsum(
            "bqhd,bhkd->bhqk",
            query_blocks,
            tile_pair[..., :head_size],
            preferred_element_type=jnp.float32,
        )
        * scaling
    )
    highest = jnp.max(scores, axis=-1)
    weights = jnp.exp(scores - highest[..., None])
    totals = jnp.sum(weights, axis=-1)
    mixed = jnp.einsum(
        "bhqk,bhkd->bhqd",
        weights.astype(jnp.bfloat16),
        tile_pair[..., head_size:],
        preferred_element_type=jnp.float32,
    )
    return (mixed, highest, totals)


def merge_parts(parts):
    top = parts[0][1]
    for part in parts[1:]:
        top = jnp.maximum(top, part[1])
    numer = jnp.zeros(parts[0][0].shape, jnp.float32)
    denom = jnp.zeros(parts[0][2].shape, jnp.float32)
    for part in parts:
        factor = jnp.exp(part[1] - top)
        numer = numer + factor[..., None] * part[0]
        denom = denom + factor * part[2]
    return numer / denom[..., None]


def general_body(queries, new_keys, new_values, cache_keys, cache_values, selection):
    heads_q, heads_k, heads_v = (
        lax.all_to_all(queries, ("heads", "sub"), split_axis=1, concat_axis=0, tiled=True),
        lax.all_to_all(new_keys, ("heads", "sub"), split_axis=1, concat_axis=0, tiled=True),
        lax.all_to_all(new_values, ("heads", "sub"), split_axis=1, concat_axis=0, tiled=True),
    )
    qblocks, head_count, top_count = selection.shape
    head_size = HD
    scaling = head_size ** (-0.5)
    shaped = (qblocks, BLOCK, head_count, head_size)
    query_blocks = heads_q.reshape(shaped)
    own = own_partial(query_blocks, heads_k.reshape(shaped), heads_v.reshape(shaped), scaling)
    seq_count = lax.axis_size("seq")
    myself = lax.axis_index("seq")
    cache_blocks = cache_keys.shape[0] // BLOCK
    tile_count = cache_blocks * head_count
    request_count = qblocks * head_count * top_count
    capacity = -(-request_count // seq_count)
    requests_all = lax.all_gather(selection, "seq", axis=0, tiled=True).reshape(
        seq_count, request_count
    )
    head_of = jnp.arange(request_count) // top_count % head_count
    my_requests = selection.reshape(request_count)
    my_owner = my_requests // cache_blocks
    my_slot = my_owner * capacity + order_ranks(my_owner)
    key_tiles = cache_keys.reshape(cache_blocks, BLOCK, head_count, head_size).transpose(0, 2, 1, 3)
    value_tiles = cache_values.reshape(cache_blocks, BLOCK, head_count, head_size).transpose(
        0, 2, 1, 3
    )
    tile_set = jnp.concatenate([key_tiles, value_tiles], axis=-1).reshape(
        tile_count, BLOCK, 2 * head_size
    )
    their_owner = requests_all // cache_blocks
    local_tile = requests_all % cache_blocks * head_count + head_of[None, :]
    served = (their_owner == myself).astype(jnp.float32)
    slot_pick = one_hot(order_ranks(their_owner), capacity) * served[..., None]
    picking = jnp.einsum("erc,erl->ecl", slot_pick, one_hot(local_tile, tile_count)).astype(
        jnp.bfloat16
    )
    parts = [own]
    outgoing = jnp.einsum(
        "ecl,lkf->eckf", picking, tile_set, preferred_element_type=jnp.float32
    ).astype(jnp.bfloat16)
    incoming = lax.all_to_all(outgoing, "seq", split_axis=0, concat_axis=0, tiled=True)
    fetched = incoming.reshape(seq_count * capacity, BLOCK, 2 * head_size)[my_slot]
    fetched = fetched.reshape(qblocks, head_count, top_count, BLOCK, 2 * head_size)
    for turn in range(top_count):
        parts.append(tile_partial(query_blocks, fetched[:, :, turn], scaling))
    result = merge_parts(parts)
    result = (
        result.transpose(0, 2, 1, 3)
        .reshape(qblocks * BLOCK, head_count * head_size)
        .astype(jnp.bfloat16)
    )
    return lax.all_to_all(result, ("heads", "sub"), split_axis=0, concat_axis=1, tiled=True)


def body(queries, new_keys, new_values, cache_keys, cache_values, selection):
    qblocks, head_count, top_count = selection.shape
    blocks_total = cache_keys.shape[0] // BLOCK * lax.axis_size("seq")
    if blocks_total == top_count and qblocks == 1:
        return dense_body(queries, new_keys, new_values, cache_keys, cache_values)
    return general_body(queries, new_keys, new_values, cache_keys, cache_values, selection)


def solution(mesh):
    in_specs = (
        P(("groups", "seq", "heads", "sub"), None),
        P(("groups", "seq", "heads", "sub"), None),
        P(("groups", "seq", "heads", "sub"), None),
        P(("groups", "seq"), ("heads", "sub")),
        P(("groups", "seq"), ("heads", "sub")),
        P(("groups", "seq"), ("heads", "sub"), None),
    )
    out_specs = P(("groups", "seq", "heads", "sub"), None)
    return jax.shard_map(body, mesh=mesh, in_specs=in_specs, out_specs=out_specs, check_vma=False)
```

profile of v0, /device:TPU:0, one launch (start us, length us, event | category | flops | bytes accessed | tf_op | source)
XLA Modules:
  0.0 74.4 jit_solution(14461604514150372851)
XLA Ops:
  0.0 72.5 %shard_map.55 = bf16[128,2048]{1,0:T(8,128)(2,1)} custom-call(bf16[128,2048]{1,0:T(8,128)(2,1)} %q_ref.1, bf16[128,2048]{1,0:T(8,128)(2,1)} %k_ref.1, bf16[128,2048]{1,0:T(8,128)(2,1)} %v_ref.1, bf16[1024,512]{1,0:T(8,128)(2,1)} %ck_ref.1, bf16[1024,512]{1,0:T(8,128)(2,1)} %cv_ref.1), custom_call_target="tpu_custom_call" | custom-call | tf_op jit(solution)/shard_map/pallas_call | solution.py:448
  72.5 1.9 %copy.7 = bf16[128,2048]{1,0:T(8,128)(2,1)} copy(bf16[128,2048]{1,0:T(8,128)(2,1)} %shard_map.55) | data formatting | bytes 1048576
where the time goes:
time: 74.6 us; the launch traced here: 74.4 us
  Pallas kernels  72.5 us (97%)
  local copies, waits for them, and re-layouts  1.88 us (3%)
    pallas_call x1, Pallas kernels, dense_body(): pl.pallas_call(functools.partial(fused_kernel, seq_count, heads_size, sub...  72.5 us
    unnamed x1, local copies, waits for them, and re-layouts  1.88 us

commit v1 on v0

--- a/solution.py
+++ b/solution.py
@@ -1,4 +1,5 @@
 import functools
+import heapq
 import math
 
 import jax
@@ -13,8 +14,144 @@
 
 
 MESH = pl.DeviceIdType.MESH
-AHEAD = 2
 TILE = 256
+
+READY, PASS, TAKE, WORK, LOAD, OWN, FOLD, EMIT, DONE, REST = range(10)
+KINDS = 16
+SEND, UNIT, SPAN, MERGE, CLOSE, WIRE, HOP = 0.06, 1.0, 0.45, 0.3, 0.4, 1.43, 2.0
+FIRST, EACH, LATE, DEEP = 2.0, 0.7, 21.0, 2
+
+
+def plan_steps(count, chunks):
+    steps = [[] for _ in range(count)]
+    free = [0.0] * count
+    seen, back = ([{} for _ in range(count)] for _ in range(2))
+    touched, passed, worked, owned, folded, emitted, finished = (
+        [set() for _ in range(count)] for _ in range(7)
+    )
+    wires = {(s, d): [] for s in range(count) for d in (-1, 1) if 0 <= s + d < count}
+    heap = []
+    for s in range(count):
+        for n in range(chunks):
+            seen[s][s, n] = FIRST + EACH * n
+            heapq.heappush(heap, (seen[s][s, n], s))
+        heapq.heappush(heap, (LATE, s))
+
+    def first_use(s, o, n):
+        if (o, n) not in touched[s]:
+            touched[s].add((o, n))
+            steps[s].append((READY if o == s else TAKE, o, n, 0))
+
+    def launch(t, s, d, arrive, entry):
+        finish = max([t] + wires[s, d][-1:]) + WIRE
+        wires[s, d].append(finish)
+        arrive[s + d][entry] = finish + HOP
+        heapq.heappush(heap, (finish + HOP, s + d))
+        heapq.heappush(heap, (finish, s))
+
+    def next_send(t, s, d):
+        found = []
+        for (o, n), when in seen[s].items():
+            onward = o == s or (o < s) == (d > 0)
+            if when <= t and onward and (o, n, d) not in passed[s]:
+                left = count - 1 - s if d > 0 else s
+                found.append((n - left + (3.0 if o == s else 0.0), 0, o, n))
+        for o, n in folded[s]:
+            if (o - s) * d > 0 and (o, n) not in emitted[s]:
+                found.append((n + 8.0 - 2.0 * abs(o - s), 1, o, n))
+        return min(found) if found else None
+
+    def next_work(t, s):
+        found = []
+        for o, n in worked[s]:
+            if o != s and (o, n) not in folded[s]:
+                far = s + (s - o) // abs(s - o)
+                if not 0 <= far < count or back[s].get((o, n), t + 1) <= t:
+                    found.append((0, n - 2 * abs(o - s), FOLD, o, n, MERGE))
+        for n in range(chunks):
+            if (s, n) in worked[s] and n in owned[s] and n not in finished[s]:
+                sides = [d for d in (-1, 1) if (s, d) in wires]
+                if all(back[s].get((s, n, d), t + 1) <= t for d in sides):
+                    found.append((1, n, DONE, s, n, CLOSE))
+        for (o, n), when in seen[s].items():
+            if when <= t and (o, n) not in worked[s]:
+                found.append((2, n - abs(o - s), WORK, o, n, UNIT))
+        if t >= LATE:
+            for n in range(chunks):
+                if n not in owned[s] and (s, n) in worked[s]:
+                    found.append((2, n + 3.5, OWN, s, n, SPAN))
+        return min(found) if found else None
+
+    while heap:
+        t, s = heapq.heappop(heap)
+        if t < free[s] - 1e-9:
+            continue
+        for d in (-1, 1):
+            while (s, d) in wires and sum(f > t for f in wires[s, d]) < DEEP:
+                best = next_send(t, s, d)
+                if best is None:
+                    break
+                _, out, o, n = best
+                if out:
+                    emitted[s].add((o, n))
+                    steps[s].append((EMIT, o, n, d))
+                    launch(t, s, d, back, (o, n, -d) if s + d == o else (o, n))
+                else:
+                    first_use(s, o, n)
+                    passed[s].add((o, n, d))
+                    steps[s].append((PASS, o, n, d))
+                    launch(t, s, d, seen, (o, n))
+                t += SEND
+        best = next_work(t, s)
+        free[s] = t
+        if best is None:
+            continue
+        _, _, kind, o, n, price = best
+        if kind == WORK:
+            first_use(s, o, n)
+            worked[s].add((o, n))
+        elif kind == OWN:
+            if not owned[s]:
+                steps[s].append((LOAD, o, n, 0))
+            owned[s].add(n)
+        elif kind == FOLD:
+            folded[s].add((o, n))
+        else:
+            finished[s].add(n)
+        steps[s].append((kind, o, n, 0))
+        free[s] = t + price
+        heapq.heappush(heap, (free[s], s))
+    return steps
+
+
+def plan_codes(count, chunks):
+    steps = plan_steps(count, chunks)
+    codes = []
+    for s, one in enumerate(steps):
+        row = [
+            k + KINDS * ((d > 0) + 2 * (o + count * n))
+            for k, o, n, d in one
+            if not (o == s and n == 0 and k in (READY, PASS))
+        ]
+        codes.append(row)
+    base = KINDS * 2 * count * chunks
+    each = max(k for k in range(1, 8) if base**k < 2**31)
+    longest = -(-max(len(row) for row in codes) // each)
+    words = []
+    for row in codes:
+        row = row + [REST] * (longest * each - len(row))
+        words.append(
+            [sum(row[w * each + k] * base**k for k in range(each)) for w in range(longest)]
+        )
+    return words, base, each
+
+
+def pick_word(words, index):
+    if len(words) == 1:
+        return words[0]
+    half = 1 << (len(words) - 1).bit_length() - 1
+    low, high = words[:half], words[half:]
+    return jnp.where(index >= half, pick_word(high, index - half), pick_word(low, index))
 
 
 def span_tile(rows, length):
@@ -82,6 +219,13 @@
     ]
     for copy in (own[0], own[4], own[3], own[1], own[2]):
         copy.start()
+    plans, base, each = plan_codes(seq_count, chunks)
+    words = []
+    for index in range(len(plans[0])):
+        value = jnp.int32(plans[0][index])
+        for s in range(1, seq_count):
+            value = jnp.where(at_seq == s, jnp.int32(plans[s][index]), value)
+        words.append(value)
     sides = has_left.astype(jnp.int32) + has_right.astype(jnp.int32)
     pl.semaphore_wait(barrier, peers - 1 + sides)
 
@@ -198,14 +342,13 @@
             def _(peer=peer):
                 landed_q(peer, chunk // halves).wait_recv()
 
-        for direction, there in ((0, has_left), (1, has_right)):
-            @pl.when(there)
-            def _(direction=direction):
-                pass_q(at_seq, chunk, direction).start()
-
     own[0].wait()
-    for chunk in range(min(AHEAD, chunks)):
-        own_ready(chunk)
+    own_ready(0)
+    for direction, there in ((0, has_left), (1, has_right)):
+        @pl.when(there)
+        def _(direction=direction):
+            pass_q(at_seq, 0, direction).start()
+
     own[4].wait()
 
     @functools.partial(each_head)
@@ -296,8 +439,9 @@
     def take_in(slot, owner, chunk):
         for copy in got_out(slot, chunk):
             copy.wait_recv()
-        mixed = msg_in[slot, chunk].astype(jnp.float32) * unfold_stats(slot, chunk, 2)
-        other = (mixed, unfold_stats(slot, chunk, 0), unfold_stats(slot, chunk, 1))
+        mixed = msg_in[slot, chunk].astype(jnp.float32) * unfold_stats(slot, chunk, 1)
+        level = unfold_stats(slot, chunk, 0)
+        other = (mixed, level, jnp.ones_like(level))
         put_part(owner, chunk, join(get_part(owner, chunk), other))
 
     def inside(index, limit):
@@ -308,94 +452,111 @@
         direction = lax.rem(index, 2)
         return at_seq + (2 * direction - 1) * distance, direction, distance
 
-    last = 2 * seq_count - 3
-
-    @pl.loop(0, chunks + last)
-    def _(turn):
-        @pl.loop(0, 2 * (seq_count - 1))
-        def _(index):
-            owner, direction, distance = foreign(index)
-            chunk = turn + 1 - distance
-
-            @pl.when(jnp.logical_and(inside(owner, seq_count), inside(chunk, chunks)))
+    def fold(owner, chunk):
+        right = (owner > at_seq).astype(jnp.int32)
+
+        @pl.when(inside(at_seq - 2 * right + 1, seq_count))
+        def _():
+            take_in(owner + right, owner, chunk)
+
+        mixed = part[owner, chunk]
+        total = pst[owner, chunk, 1:2]
+        most = jnp.maximum(jnp.max(jnp.abs(mixed), axis=0, keepdims=True), 1e-30)
+        msg_out[owner, chunk] = (
+            jnp.round(mixed * (32767.0 / most)).astype(jnp.int32).astype(jnp.int16)
+        )
+        fold_stats(owner, chunk, 0, pst[owner, chunk, 0:1] + jnp.log2(total))
+        fold_stats(owner, chunk, 1, most * (1.0 / 32767.0) / total)
+
+    def load():
+        own[1].wait()
+        own[2].wait()
+        for which in range(2):
+            for step in range(1, peers):
+                peer = peer_of(step)
+                spread_kv(which, peer, peer).wait_recv()
+
+    def close(chunk):
+        head = chunk // halves
+        for side, there in ((1, has_left), (0, has_right)):
+            @pl.when(there)
+            def _(side=side):
+                take_in(at_seq + side, at_seq, chunk)
+
+        done = part[at_seq, chunk] / pst[at_seq, chunk, 1:2]
+        fin[span_of(chunk), columns(head)] = done.T.astype(jnp.bfloat16)
+        for index in range(bands):
+            peer = lax.rem(chunk, halves) * bands + index
+
+            @pl.when(peer != place)
+            def _(peer=peer):
+                spread_out(peer, place, head).start()
+
+            @pl.when(peer == place)
+            def _():
+                keep_out(head).start()
+
+    def emit(owner, chunk):
+        for copy in pass_out(owner, chunk, (owner > at_seq).astype(jnp.int32)):
+            copy.start()
+
+    def step(code):
+        kind, rest = lax.rem(code, KINDS), code // KINDS
+        direction, rest = lax.rem(rest, 2), rest // 2
+        owner, chunk = lax.rem(rest, seq_count), rest // seq_count
+
+        @pl.when(kind <= TAKE)
+        def _():
+            @pl.when(kind == READY)
+            def _():
+                own_ready(chunk)
+
+            @pl.when(kind == TAKE)
             def _():
                 pass_q(owner, chunk, 0).wait_recv()
-                onward = 1 - direction
-
-                @pl.when(inside(at_seq + 2 * onward - 1, seq_count))
-                def _():
-                    pass_q(owner, chunk, onward).start()
-
-        @pl.when(turn + AHEAD < chunks)
+
+            @pl.when(kind == PASS)
+            def _():
+                pass_q(owner, chunk, direction).start()
+
+        @pl.when(jnp.logical_and(kind > TAKE, kind <= OWN))
         def _():
-            own_ready(turn + AHEAD)
-
-        @pl.loop(0, 2 * (seq_count - 1))
-        def _(back):
-            owner, direction, distance = foreign(2 * (seq_count - 1) - 1 - back)
-            chunk = turn + 1 - distance
-
-            @pl.when(jnp.logical_and(inside(owner, seq_count), inside(chunk, chunks)))
+            @pl.when(kind == WORK)
             def _():
                 cached_part(owner, chunk)
 
-            chunk = turn - (last - distance)
-
-            @pl.when(jnp.logical_and(inside(owner, seq_count), inside(chunk, chunks)))
-            def _():
-                @pl.when(inside(at_seq - 2 * direction + 1, seq_count))
-                def _():
-                    take_in(owner + direction, owner, chunk)
-
-                mixed = part[owner, chunk]
-                most = jnp.maximum(jnp.max(jnp.abs(mixed), axis=0, keepdims=True), 1e-30)
-                msg_out[owner, chunk] = (
-                    jnp.round(mixed * (32767.0 / most)).astype(jnp.int32).astype(jnp.int16)
-                )
-                fold_stats(owner, chunk, 0, pst[owner, chunk, 0:1])
-                fold_stats(owner, chunk, 1, pst[owner, chunk, 1:2])
-                fold_stats(owner, chunk, 2, most * (1.0 / 32767.0))
-                for copy in pass_out(owner, chunk, direction):
-                    copy.start()
-
-        @pl.when(turn < chunks)
+            @pl.when(kind == LOAD)
+            def _():
+                load()
+
+            @pl.when(kind == OWN)
+            def _():
+                own_part(chunk)
+
+        @pl.when(kind > OWN)
         def _():
-            cached_part(at_seq, turn)
-
-        @pl.when(turn == last - 1)
-        def _():
-            own[1].wait()
-            own[2].wait()
-            for which in range(2):
-                for step in range(1, peers):
-                    peer = peer_of(step)
-                    spread_kv(which, peer, peer).wait_recv()
-
-        @pl.when(inside(turn - (last - 1), chunks))
-        def _():
-            own_part(turn - (last - 1))
-
-        @pl.when(turn >= last)
-        def _():
-            chunk = turn - last
-            head = chunk // halves
-            for side, there in ((1, has_left), (0, has_right)):
-                @pl.when(there)
-                def _(side=side):
-                    take_in(at_seq + side, at_seq, chunk)
-
-            done = part[at_seq, chunk] / pst[at_seq, chunk, 1:2]
-            fin[span_of(chunk), columns(head)] = done.T.astype(jnp.bfloat16)
-            for index in range(bands):
-                peer = lax.rem(chunk, halves) * bands + index
-
-                @pl.when(peer != place)
-                def _(peer=peer):
-                    spread_out(peer, place, head).start()
-
-                @pl.when(peer == place)
-                def _():
-                    keep_out(head).start()
+            @pl.when(kind == FOLD)
+            def _():
+                fold(owner, chunk)
+
+            @pl.when(kind == EMIT)
+            def _():
+                emit(owner, chunk)
+
+            @pl.when(kind == DONE)
+            def _():
+                close(chunk)
+
+    @pl.loop(0, len(words))
+    def _(index):
+        word = pick_word(words, index)
+
+        @pl.loop(0, each)
+        def _(field):
+            code = lax.rem(word, base)
+            for k in range(1, each):
+                code = jnp.where(field == k, lax.rem(lax.div(word, base**k), base), code)
+            step(code)
 
     @functools.partial(each_head)
     def _(head):
@@ -442,7 +603,7 @@
     tile = span_tile(rows, length)
     chunks = head_count * (length // tile)
     lanes = min(tile, 128)
-    stat_rows = -(-3 * (tile // lanes) // 8) * 8
+    stat_rows = 2 * (tile // lanes)
     dma = pltpu.SemaphoreType.DMA
     anywhere = pl.BlockSpec(memory_space=pltpu.HBM)
     return pl.pallas_call(

time: 74.6 us -> 70 us (0.938)
  Pallas kernels: 72.5 us -> 67.2 us
    pallas_call x1, Pallas kernels: 72.5 us -> 67.2 us  [dense_body(): pl.pallas_call(functools.partial(fused_kernel, seq_count, heads_size, sub...]
where the time goes in v1:
time: 70 us; the launch traced here: 69.1 us
  Pallas kernels  67.2 us (96%)
  local copies, waits for them, and re-layouts  1.88 us (3%)
    pallas_call x1, Pallas kernels, dense_body(): pl.pallas_call(functools.partial(fused_kernel, seq_count, heads_size, sub...  67.2 us
    unnamed x1, local copies, waits for them, and re-layouts  1.88 us

profile of v1, /device:TPU:0, one launch (start us, length us, event | category | flops | bytes accessed | tf_op | source)
XLA Modules:
  0.0 69.1 jit_solution(11366560513985133170)
XLA Ops:
  0.0 67.2 %shard_map.55 = bf16[128,2048]{1,0:T(8,128)(2,1)} custom-call(bf16[128,2048]{1,0:T(8,128)(2,1)} %q_ref.1, bf16[128,2048]{1,0:T(8,128)(2,1)} %k_ref.1, bf16[128,2048]{1,0:T(8,128)(2,1)} %v_ref.1, bf16[1024,512]{1,0:T(8,128)(2,1)} %ck_ref.1, bf16[1024,512]{1,0:T(8,128)(2,1)} %cv_ref.1), custom_call_target="tpu_custom_call" | custom-call | tf_op jit(solution)/shard_map/pallas_call | solution.py:609
  67.2 1.9 %copy.7 = bf16[128,2048]{1,0:T(8,128)(2,1)} copy(bf16[128,2048]{1,0:T(8,128)(2,1)} %shard_map.55) | data formatting | bytes 1048576

commit v2 on v1

--- a/solution.py
+++ b/solution.py
@@ -15,14 +15,16 @@
 
 MESH = pl.DeviceIdType.MESH
 TILE = 256
-
-READY, PASS, TAKE, WORK, LOAD, OWN, FOLD, EMIT, DONE, REST = range(10)
+KEYS = 256
+
+READY, TAKE, PASS, START, RELAY, WORK, OWN, LOAD, FOLD, EMIT, DONE, REST = range(12)
 KINDS = 16
-SEND, UNIT, SPAN, MERGE, CLOSE, WIRE, HOP = 0.06, 1.0, 0.45, 0.3, 0.4, 1.43, 2.0
-FIRST, EACH, LATE, DEEP = 2.0, 0.7, 21.0, 2
-
-
-def plan_steps(count, chunks):
+SEND, UNIT, SPAN, MERGE, CLOSE, WIRE, HOP = 0.08, 0.68, 0.35, 0.28, 0.4, 1.43, 2.0
+FIRST, EACH, LATE, DEEP = 2.0, 0.7, 21.0, 3
+K_FAR, K_OUT, K_DIST, K_OWN, W_DIST, W_SELF, W_OWN = 1.0, 8.0, 2.0, 3.0, 1.0, 0.0, 3.5
+
+
+def plan_steps(count, chunks, group):
     steps = [[] for _ in range(count)]
     free = [0.0] * count
     seen, back = ([{} for _ in range(count)] for _ in range(2))
@@ -55,10 +57,10 @@
             onward = o == s or (o < s) == (d > 0)
             if when <= t and onward and (o, n, d) not in passed[s]:
                 left = count - 1 - s if d > 0 else s
-                found.append((n - left + (3.0 if o == s else 0.0), 0, o, n))
+                found.append((n - K_FAR * left + (K_OWN if o == s else 0.0), 0, o, n))
         for o, n in folded[s]:
             if (o - s) * d > 0 and (o, n) not in emitted[s]:
-                found.append((n + 8.0 - 2.0 * abs(o - s), 1, o, n))
+                found.append((n + K_OUT - K_DIST * abs(o - s), 1, o, n))
         return min(found) if found else None
 
     def next_work(t, s):
@@ -73,13 +75,14 @@
                 sides = [d for d in (-1, 1) if (s, d) in wires]
                 if all(back[s].get((s, n, d), t + 1) <= t for d in sides):
                     found.append((1, n, DONE, s, n, CLOSE))
-        for (o, n), when in seen[s].items():
-            if when <= t and (o, n) not in worked[s]:
-                found.append((2, n - abs(o - s), WORK, o, n, UNIT))
-        if t >= LATE:
-            for n in range(chunks):
-                if n not in owned[s] and (s, n) in worked[s]:
-                    found.append((2, n + 3.5, OWN, s, n, SPAN))
+        for n in range(0, chunks, group):
+            for o in range(count):
+                here = all(seen[s].get((o, n + k), t + 1) <= t for k in range(group))
+                if here and (o, n) not in worked[s]:
+                    rank = n - (W_DIST * abs(o - s) if o != s else W_SELF)
+                    found.append((2, rank, WORK, o, n, UNIT * group))
+            if t >= LATE and n not in owned[s] and (s, n) in worked[s]:
+                found.append((2, n + W_OWN, OWN, s, n, SPAN * group))
         return min(found) if found else None
 
     while heap:
@@ -108,12 +111,13 @@
             continue
         _, _, kind, o, n, price = best
         if kind == WORK:
-            first_use(s, o, n)
-            worked[s].add((o, n))
+            for k in range(group):
+                first_use(s, o, n + k)
+                worked[s].add((o, n + k))
         elif kind == OWN:
             if not owned[s]:
                 steps[s].append((LOAD, o, n, 0))
-            owned[s].add(n)
+            owned[s].update(range(n, n + group))
         elif kind == FOLD:
             folded[s].add((o, n))
         else:
@@ -124,15 +128,23 @@
     return steps
 
 
-def plan_codes(count, chunks):
-    steps = plan_steps(count, chunks)
+def join_steps(steps):
+    joined = []
+    for kind, o, n, d in steps:
+        if kind == PASS and joined and joined[-1][1:3] == (o, n):
+            if joined[-1][0] in (READY, TAKE):
+                joined[-1] = (START if joined[-1][0] == READY else RELAY, o, n, d)
+                continue
+        joined.append((kind, o, n, d))
+    return joined
+
+
+def plan_codes(count, chunks, group):
+    steps = plan_steps(count, chunks, group)
     codes = []
     for s, one in enumerate(steps):
-        row = [
-            k + KINDS * ((d > 0) + 2 * (o + count * n))
-            for k, o, n, d in one
-            if not (o == s and n == 0 and k in (READY, PASS))
-        ]
+        one = [x for x in one if not (x[1:3] == (s, 0) and x[0] in (READY, PASS))]
+        row = [k + KINDS * ((d > 0) + 2 * (o + count * n)) for k, o, n, d in join_steps(one)]
         codes.append(row)
     base = KINDS * 2 * count * chunks
     each = max(k for k in range(1, 8) if base**k < 2**31)
@@ -219,7 +231,7 @@
     ]
     for copy in (own[0], own[4], own[3], own[1], own[2]):
         copy.start()
-    plans, base, each = plan_codes(seq_count, chunks)
+    plans, base, each = plan_codes(seq_count, chunks, halves)
     words = []
     for index in range(len(plans[0])):
         value = jnp.int32(plans[0][index])
@@ -264,7 +276,7 @@
         return pl.ds(pl.multiple_of(lax.rem(chunk, halves) * tile, tile), tile)
 
     def pass_q(owner, chunk, direction):
-        piece = qall.at[owner, span_of(chunk), columns(chunk // halves)]
+        piece = qall.at[owner, span_of(chunk), columns(lax.div(chunk, halves))]
         return pltpu.make_async_remote_copy(
             src_ref=piece,
             dst_ref=piece,
@@ -340,7 +352,7 @@
 
             @pl.when(peer != place)
             def _(peer=peer):
-                landed_q(peer, chunk // halves).wait_recv()
+                landed_q(peer, lax.div(chunk, halves)).wait_recv()
 
     own[0].wait()
     own_ready(0)
@@ -361,19 +373,31 @@
 
     own[3].wait()
 
-    def attend(keys, values_t, queries, causal):
-        scores = lax.dot_general(
-            keys, queries, (((1,), (1,)), ((), ())), preferred_element_type=jnp.float32
-        )
-        if causal is not None:
-            scores = jnp.where(causal, scores, -jnp.inf)
-        top = jnp.max(scores, axis=0, keepdims=True)
-        weights = jnp.exp2((scores - top) * scaling)
-        total = jnp.sum(weights, axis=0, keepdims=True)
-        mixed = jnp.dot(
-            values_t, weights.astype(jnp.bfloat16), preferred_element_type=jnp.float32
-        )
-        return mixed, top * scaling, total
+    def attend(keys, values_t, queries, causal=None):
+        count = keys.shape[0] // KEYS
+        scores = []
+        for at in range(count):
+            score = lax.dot_general(
+                keys[at * KEYS:(at + 1) * KEYS],
+                queries,
+                (((1,), (1,)), ((), ())),
+                preferred_element_type=jnp.float32,
+            )
+            if causal is not None:
+                score = jnp.where(causal[at * KEYS:(at + 1) * KEYS], score, -jnp.inf)
+            scores.append(score)
+        tops = [jnp.max(score, axis=0, keepdims=True) for score in scores]
+        top = functools.reduce(jnp.maximum, tops) * scaling
+        mixed = total = 0.0
+        for at, score in enumerate(scores):
+            weights = jnp.exp2(score * scaling - top)
+            total = total + jnp.sum(weights, axis=0, keepdims=True)
+            mixed = mixed + jnp.dot(
+                values_t[:, at * KEYS:(at + 1) * KEYS],
+                weights.astype(jnp.bfloat16),
+                preferred_element_type=jnp.float32,
+            )
+        return mixed, top, total
 
     def join(a, b):
         top = jnp.maximum(a[1], b[1])
@@ -389,36 +413,23 @@
         return part[owner, chunk], pst[owner, chunk, 0:1], pst[owner, chunk, 1:2]
 
     def cached_part(owner, chunk):
-        head = chunk // halves
-        queries = qall[owner, span_of(chunk), columns(head)]
-        result = None
-        for block in range(cache_blocks):
-            piece = attend(
-                kc[block * BLOCK:(block + 1) * BLOCK, columns(head)],
-                vt[head, :, block * BLOCK:(block + 1) * BLOCK],
-                queries,
-                None,
-            )
-            result = piece if result is None else join(result, piece)
-        put_part(owner, chunk, result)
+        head = lax.div(chunk, halves)
+        keys, values_t = kc[:, columns(head)], vt[head]
+        for at in range(halves):
+            queries = qall[owner, at * tile:(at + 1) * tile, columns(head)]
+            put_part(owner, chunk + at, attend(keys, values_t, queries))
 
     def own_part(chunk):
-        head = chunk // halves
-        queries = qall[at_seq, span_of(chunk), columns(head)]
+        head = lax.div(chunk, halves)
+        keys = kown[:, columns(head)]
+        values_t = vown[:, columns(head)].astype(jnp.float32).T.astype(jnp.bfloat16)
         for at in range(halves):
-            @pl.when(lax.rem(chunk, halves) == at)
-            def _(at=at):
-                depth = (at + 1) * tile
-                key_at = lax.broadcasted_iota(jnp.int32, (depth, tile), 0)
-                query_at = lax.broadcasted_iota(jnp.int32, (depth, tile), 1) + at * tile
-                values_t = vown[0:depth, columns(head)].astype(jnp.float32).T
-                piece = attend(
-                    kown[0:depth, columns(head)],
-                    values_t.astype(jnp.bfloat16),
-                    queries,
-                    key_at <= query_at,
-                )
-                put_part(at_seq, chunk, join(piece, get_part(at_seq, chunk)))
+            depth = (at + 1) * tile
+            key_at = lax.broadcasted_iota(jnp.int32, (depth, tile), 0)
+            query_at = lax.broadcasted_iota(jnp.int32, (depth, tile), 1) + at * tile
+            queries = qall[at_seq, at * tile:(at + 1) * tile, columns(head)]
+            piece = attend(keys[0:depth], values_t[:, 0:depth], queries, key_at <= query_at)
+            put_part(at_seq, chunk + at, join(piece, get_part(at_seq, chunk + at)))
 
     lanes = min(tile, 128)
     folds = tile // lanes
@@ -477,7 +488,7 @@
                 spread_kv(which, peer, peer).wait_recv()
 
     def close(chunk):
-        head = chunk // halves
+        head = lax.div(chunk, halves)
         for side, there in ((1, has_left), (0, has_right)):
             @pl.when(there)
             def _(side=side):
@@ -501,39 +512,39 @@
             copy.start()
 
     def step(code):
-        kind, rest = lax.rem(code, KINDS), code // KINDS
-        direction, rest = lax.rem(rest, 2), rest // 2
-        owner, chunk = lax.rem(rest, seq_count), rest // seq_count
-
-        @pl.when(kind <= TAKE)
+        kind, rest = lax.rem(code, KINDS), lax.div(code, KINDS)
+        direction, rest = lax.rem(rest, 2), lax.div(rest, 2)
+        owner, chunk = lax.rem(rest, seq_count), lax.div(rest, seq_count)
+
+        @pl.when(kind <= RELAY)
         def _():
-            @pl.when(kind == READY)
+            @pl.when(jnp.logical_or(kind == READY, kind == START))
             def _():
                 own_ready(chunk)
 
-            @pl.when(kind == TAKE)
+            @pl.when(jnp.logical_or(kind == TAKE, kind == RELAY))
             def _():
                 pass_q(owner, chunk, 0).wait_recv()
 
-            @pl.when(kind == PASS)
+            @pl.when(kind >= PASS)
             def _():
                 pass_q(owner, chunk, direction).start()
 
-        @pl.when(jnp.logical_and(kind > TAKE, kind <= OWN))
+        @pl.when(jnp.logical_and(kind > RELAY, kind < FOLD))
         def _():
             @pl.when(kind == WORK)
             def _():
                 cached_part(owner, chunk)
 
+            @pl.when(kind == OWN)
+            def _():
+                own_part(chunk)
+
             @pl.when(kind == LOAD)
             def _():
                 load()
 
-            @pl.when(kind == OWN)
-            def _():
-                own_part(chunk)
-
-        @pl.when(kind > OWN)
+        @pl.when(kind >= FOLD)
         def _():
             @pl.when(kind == FOLD)
             def _():

time: 70 us -> 65.2 us (0.931); the launches traced: 69.1 us -> 65.1 us
  Pallas kernels: 67.2 us -> 63.2 us
    pallas_call x1, Pallas kernels: 67.2 us -> 63.2 us  [dense_body(): pl.pallas_call(functools.partial(fused_kernel, seq_count, heads_size, sub...]
where the time goes in v2:
time: 65.2 us; the launch traced here: 65.1 us
  Pallas kernels  63.2 us (97%)
  local copies, waits for them, and re-layouts  1.88 us (3%)
    pallas_call x1, Pallas kernels, dense_body(): pl.pallas_call(functools.partial(fused_kernel, seq_count, heads_size, sub...  63.2 us
    unnamed x1, local copies, waits for them, and re-layouts  1.88 us

profile of v2, /device:TPU:0, one launch (start us, length us, event | category | flops | bytes accessed | tf_op | source)
XLA Modules:
  0.0 65.1 jit_solution(13059240067575874175)
XLA Ops:
  0.0 63.2 %shard_map.55 = bf16[128,2048]{1,0:T(8,128)(2,1)} custom-call(bf16[128,2048]{1,0:T(8,128)(2,1)} %q_ref.1, bf16[128,2048]{1,0:T(8,128)(2,1)} %k_ref.1, bf16[128,2048]{1,0:T(8,128)(2,1)} %v_ref.1, bf16[1024,512]{1,0:T(8,128)(2,1)} %ck_ref.1, bf16[1024,512]{1,0:T(8,128)(2,1)} %cv_ref.1), custom_call_target="tpu_custom_call" | custom-call | tf_op jit(solution)/shard_map/pallas_call | solution.py:620
  63.2 1.9 %copy.7 = bf16[128,2048]{1,0:T(8,128)(2,1)} copy(bf16[128,2048]{1,0:T(8,128)(2,1)} %shard_map.55) | data formatting | bytes 1048576

commit v3 on v2

--- a/solution.py
+++ b/solution.py
@@ -19,9 +19,10 @@
 
 READY, TAKE, PASS, START, RELAY, WORK, OWN, LOAD, FOLD, EMIT, DONE, REST = range(12)
 KINDS = 16
-SEND, UNIT, SPAN, MERGE, CLOSE, WIRE, HOP = 0.08, 0.68, 0.35, 0.28, 0.4, 1.43, 2.0
-FIRST, EACH, LATE, DEEP = 2.0, 0.7, 21.0, 3
-K_FAR, K_OUT, K_DIST, K_OWN, W_DIST, W_SELF, W_OWN = 1.0, 8.0, 2.0, 3.0, 1.0, 0.0, 3.5
+SEND, UNIT, SPAN, MERGE, CLOSE, WIRE, HOP = 0.08, 0.78, 0.35, 0.37, 0.4, 1.43, 3.15
+FIRST, EACH, LATE, DEEP = 0.81, 0.7, 20.42, 2
+FAR = 2.48
+K_FAR, K_OUT, K_DIST, K_OWN, W_DIST, W_SELF, W_OWN = 4.45, 10.85, -0.77, 4.61, 1.08, 7.29, 3.32
 
 
 def plan_steps(count, chunks, group):
@@ -35,7 +36,7 @@
     heap = []
     for s in range(count):
         for n in range(chunks):
-            seen[s][s, n] = FIRST + EACH * n
+            seen[s][s, n] = FIRST if n % group == 0 else FAR + EACH * n
             heapq.heappush(heap, (seen[s][s, n], s))
         heapq.heappush(heap, (LATE, s))
 
@@ -193,8 +194,18 @@
     place = lax.axis_index("heads") * sub_size + lax.axis_index("sub")
     has_left, has_right = at_seq > 0, at_seq < seq_count - 1
 
+    at_heads, at_sub = lax.axis_index("heads"), lax.axis_index("sub")
+    own_half = lax.div(place, bands)
+
     def peer_of(step):
-        return lax.rem(place + step, peers)
+        row = lax.rem(at_heads + step // sub_size, heads_size)
+        return row * sub_size + lax.rem(at_sub + step % sub_size, sub_size)
+
+    def half_of(chunk):
+        return lax.rem(chunk + own_half, halves)
+
+    def chunk_at(first, half):
+        return first + lax.rem(half + halves - own_half, halves)
 
     def peer_id(peer):
         return {"heads": peer // sub_size, "sub": lax.rem(peer, sub_size)}
@@ -273,7 +284,7 @@
         )
 
     def span_of(chunk):
-        return pl.ds(pl.multiple_of(lax.rem(chunk, halves) * tile, tile), tile)
+        return pl.ds(pl.multiple_of(half_of(chunk) * tile, tile), tile)
 
     def pass_q(owner, chunk, direction):
         piece = qall.at[owner, span_of(chunk), columns(lax.div(chunk, halves))]
@@ -348,7 +359,7 @@
 
     def own_ready(chunk):
         for index in range(bands):
-            peer = lax.rem(chunk, halves) * bands + index
+            peer = half_of(chunk) * bands + index
 
             @pl.when(peer != place)
             def _(peer=peer):
@@ -417,7 +428,7 @@
         keys, values_t = kc[:, columns(head)], vt[head]
         for at in range(halves):
             queries = qall[owner, at * tile:(at + 1) * tile, columns(head)]
-            put_part(owner, chunk + at, attend(keys, values_t, queries))
+            put_part(owner, chunk_at(chunk, at), attend(keys, values_t, queries))
 
     def own_part(chunk):
         head = lax.div(chunk, halves)
@@ -429,7 +440,8 @@
             query_at = lax.broadcasted_iota(jnp.int32, (depth, tile), 1) + at * tile
             queries = qall[at_seq, at * tile:(at + 1) * tile, columns(head)]
             piece = attend(keys[0:depth], values_t[:, 0:depth], queries, key_at <= query_at)
-            put_part(at_seq, chunk + at, join(piece, get_part(at_seq, chunk + at)))
+            slot = chunk_at(chunk, at)
+            put_part(at_seq, slot, join(piece, get_part(at_seq, slot)))
 
     lanes = min(tile, 128)
     folds = tile // lanes
@@ -497,7 +509,7 @@
         done = part[at_seq, chunk] / pst[at_seq, chunk, 1:2]
         fin[span_of(chunk), columns(head)] = done.T.astype(jnp.bfloat16)
         for index in range(bands):
-            peer = lax.rem(chunk, halves) * bands + index
+            peer = half_of(chunk) * bands + index
 
             @pl.when(peer != place)
             def _(peer=peer):
@@ -621,7 +633,7 @@
         functools.partial(fused_kernel, seq_count, heads_size, sub_size, head_count),
         out_shape=jax.ShapeDtypeStruct((rows, width), jnp.bfloat16),
         in_specs=[anywhere] * 5,
-        out_specs=pl.BlockSpec(memory_space=pltpu.VMEM),
+        out_specs=anywhere,
         scratch_shapes=[
             pltpu.VMEM((seq_count, length, span_cols), jnp.bfloat16),
             pltpu.VMEM((length, span_cols), jnp.bfloat16),

time: 65.2 us -> 61.9 us (0.949)
  Pallas kernels: 63.2 us -> 59.9 us
    pallas_call x1, Pallas kernels: 63.2 us -> 59.9 us  [dense_body(): pl.pallas_call(functools.partial(fused_kernel, seq_count, heads_size, sub...]
where the time goes in v3:
time: 61.9 us; the launch traced here: 61.7 us
  Pallas kernels  59.9 us (97%)
  local copies, waits for them, and re-layouts  1.88 us (3%)
    pallas_call x1, Pallas kernels, dense_body(): pl.pallas_call(functools.partial(fused_kernel, seq_count, heads_size, sub...  59.9 us
    unnamed x1, local copies, waits for them, and re-layouts  1.88 us

profile of v3, /device:TPU:0, one launch (start us, length us, event | category | flops | bytes accessed | tf_op | source)
XLA Modules:
  0.0 61.7 jit_solution(4578839455122315520)
XLA Ops:
  0.0 59.9 %shard_map.55 = bf16[128,2048]{1,0:T(8,128)(2,1)} custom-call(bf16[128,2048]{1,0:T(8,128)(2,1)} %q_ref.1, bf16[128,2048]{1,0:T(8,128)(2,1)} %k_ref.1, bf16[128,2048]{1,0:T(8,128)(2,1)} %v_ref.1, bf16[1024,512]{1,0:T(8,128)(2,1)} %ck_ref.1, bf16[1024,512]{1,0:T(8,128)(2,1)} %cv_ref.1), custom_call_target="tpu_custom_call" | custom-call | tf_op jit(solution)/shard_map/pallas_call | solution.py:632
  59.9 1.9 %copy.7 = bf16[128,2048]{1,0:T(8,128)(2,1)} copy(bf16[128,2048]{1,0:T(8,128)(2,1)} %shard_map.55) | data formatting | bytes 1048576

commit v4 on v3

--- a/solution.py
+++ b/solution.py
@@ -581,39 +581,43 @@
                 code = jnp.where(field == k, lax.rem(lax.div(word, base**k), base), code)
             step(code)
 
+    @pl.loop(0, chunks)
+    def _(chunk):
+        for direction, there in ((0, has_left), (1, has_right)):
+            @pl.when(there)
+            def _(direction=direction):
+                pass_q(at_seq, chunk, direction).wait_send()
+
+        @pl.loop(0, 2 * (seq_count - 1))
+        def _(index):
+            owner, direction, distance = foreign(index)
+
+            @pl.when(inside(owner, seq_count))
+            def _():
+                for copy in pass_out(owner, chunk, direction):
+                    copy.wait_send()
+                onward = 1 - direction
+
+                @pl.when(inside(at_seq + 2 * onward - 1, seq_count))
+                def _():
+                    pass_q(owner, chunk, onward).wait_send()
+
+    for which in range(2):
+        for step in range(1, peers):
+            spread_kv(which, peer_of(step), place).wait_send()
+
+    @functools.partial(each_head)
+    def _(head):
+        for step in range(1, peers):
+            spread_q(peer_of(step), head).wait_send()
+
     @functools.partial(each_head)
     def _(head):
         for step in range(1, peers):
             peer = peer_of(step)
             spread_out(peer, peer, head).wait_recv()
             spread_out(peer, place, head).wait_send()
-            spread_q(peer, head).wait_send()
         keep_out(head).wait()
-
-    @pl.loop(0, chunks)
-    def _(chunk):
-        for direction, there in ((0, has_left), (1, has_right)):
-            @pl.when(there)
-            def _(direction=direction):
-                pass_q(at_seq, chunk, direction).wait_send()
-
-        @pl.loop(0, 2 * (seq_count - 1))
-        def _(index):
-            owner, direction, distance = foreign(index)
-
-            @pl.when(inside(owner, seq_count))
-            def _():
-                for copy in pass_out(owner, chunk, direction):
-                    copy.wait_send()
-                onward = 1 - direction
-
-                @pl.when(inside(at_seq + 2 * onward - 1, seq_count))
-                def _():
-                    pass_q(owner, chunk, onward).wait_send()
-
-    for which in range(2):
-        for step in range(1, peers):
-            spread_kv(which, peer_of(step), place).wait_send()
 
 
 def dense_body(queries, new_keys, new_values, cache_keys, cache_values):

time: 61.9 us -> 60.8 us (0.982)
  Pallas kernels: 59.9 us -> 58.7 us
    pallas_call x1, Pallas kernels: 59.9 us -> 58.7 us  [dense_body(): pl.pallas_call(functools.partial(fused_kernel, seq_count, heads_size, sub...]
where the time goes in v4:
time: 60.8 us; the launch traced here: 60.6 us
  Pallas kernels  58.7 us (97%)
  local copies, waits for them, and re-layouts  1.88 us (3%)
    pallas_call x1, Pallas kernels, dense_body(): pl.pallas_call(functools.partial(fused_kernel, seq_count, heads_size, sub...  58.7 us
    unnamed x1, local copies, waits for them, and re-layouts  1.88 us

profile of v4, /device:TPU:0, one launch (start us, length us, event | category | flops | bytes accessed | tf_op | source)
XLA Modules:
  0.0 60.6 jit_solution(7013960941990301925)
XLA Ops:
  0.0 58.7 %shard_map.55 = bf16[128,2048]{1,0:T(8,128)(2,1)} custom-call(bf16[128,2048]{1,0:T(8,128)(2,1)} %q_ref.1, bf16[128,2048]{1,0:T(8,128)(2,1)} %k_ref.1, bf16[128,2048]{1,0:T(8,128)(2,1)} %v_ref.1, bf16[1024,512]{1,0:T(8,128)(2,1)} %ck_ref.1, bf16[1024,512]{1,0:T(8,128)(2,1)} %cv_ref.1), custom_call_target="tpu_custom_call" | custom-call | tf_op jit(solution)/shard_map/pallas_call | solution.py:636
  58.7 1.9 %copy.7 = bf16[128,2048]{1,0:T(8,128)(2,1)} copy(bf16[128,2048]{1,0:T(8,128)(2,1)} %shard_map.55) | data formatting | bytes 1048576
